TPU v7x, 256 devices: a whole 4x4x8 slice. The times are simulated.
256 devices in a mesh: rows: 8 (over y, core), cols: 32 (over x, z).
Axes of the slice: x: 4, y: 4, z: 8, core: 2. Of those that a mesh axis runs over, the one named last changes fastest.
Arguments:
- logged: bfloat16 [32768, 128], P(('rows', 'cols')), may hold values from -5 to 5
- targets: bfloat16 [65536, 128], P('cols'), may hold values from -5 to 5
- log_a: float32 [32768], P('rows'), may hold values from -2 to 2
- log_b: float32 [65536], P('cols'), may hold values from -2 to 2
- start_g: float32 [65536], P('cols'), may hold values from -2 to 142
Outputs:
- pot_f: float32 [32768], P('rows')
- pot_g: float32 [65536], P('cols')
All inputs are finite; a program needn't handle non-finite values.
Results may differ from a plain program's by a relative error of at most 0.0003.
Values may be sent and summed in bfloat16 or wider, within the bound.
A program may use at most 64 MiB of HBM per device.

v0:
```python
import jax
import jax.numpy as jnp
from jax import lax
from jax.sharding import PartitionSpec as P

ITERS = 3
EPS = 0.5
BLOCK = 256


def inner_cost(xb, targets, tnorm):
    xnorm = jnp.sum(jnp.square(xb.astype(jnp.float32)), axis=1)
    inner = lax.dot_general(
        xb, targets, (((1,), (1,)), ((), ())), preferred_element_type=jnp.float32
    )
    return xnorm[:, None] + tnorm[None, :] - 2.0 * inner


def row_partial(x_piece, targets, tnorm, log_b, pot_g):

    def one(xb):
        cost = inner_cost(xb, targets, tnorm)
        s = log_b[None, :] + (pot_g[None, :] - cost) / EPS
        top = jnp.max(s, axis=1)
        total = jnp.sum(jnp.exp(s - top[:, None]), axis=1)
        return jnp.stack([top, total])

    count = x_piece.shape[0]
    parts = lax.map(one, x_piece.reshape(count // BLOCK, BLOCK, x_piece.shape[1]))
    return jnp.transpose(parts, (1, 0, 2)).reshape(2, count)


def col_update(carry, x_piece, f_piece, a_piece, targets, tnorm):

    def step(state, item):
        xb, fb, ab = item
        cost = inner_cost(xb, targets, tnorm)
        s = ab[:, None] + (fb[:, None] - cost) / EPS
        upper = jnp.maximum(state[0], jnp.max(s, axis=0))
        total = state[1] * jnp.exp(state[0] - upper) + jnp.sum(jnp.exp(s - upper[None, :]), axis=0)
        return ((upper, total), None)

    count = x_piece.shape[0]
    blocks = count // BLOCK
    items = (
        x_piece.reshape(blocks, BLOCK, x_piece.shape[1]),
        f_piece.reshape(blocks, BLOCK),
        a_piece.reshape(blocks, BLOCK),
    )
    result, unused = lax.scan(step, carry, items)
    return result


def join_cols(top, total):
    upper = lax.pmax(top, "cols")
    whole = lax.psum(total * jnp.exp(top - upper), "cols")
    return -EPS * (upper + jnp.log(whole))


def join_rows(top, total):
    upper = lax.pmax(top, "rows")
    whole = lax.psum(total * jnp.exp(top - upper), "rows")
    return -EPS * (upper + jnp.log(whole))


def local(logged, targets, log_a, log_b, start_g):
    tnorm = jnp.sum(jnp.square(targets.astype(jnp.float32)), axis=1)
    width = targets.shape[0]
    pot_g = start_g
    pot_f = jnp.zeros(log_a.shape, jnp.float32)
    gathered = lax.all_gather(logged, "cols", axis=0, tiled=True)
    for step in range(ITERS):
        partial_value = row_partial(gathered, targets, tnorm, log_b, pot_g)
        pot_f = join_cols(partial_value[0], partial_value[1])
        init = (jnp.full((width,), -1e30, jnp.float32), jnp.zeros((width,), jnp.float32))
        top, total = col_update(init, gathered, pot_f, log_a, targets, tnorm)
        pot_g = join_rows(top, total)
    return (pot_f, pot_g)


def solution(mesh):
    placed = (P(("rows", "cols"), None), P("cols", None), P("rows"), P("cols"), P("cols"))
    return jax.shard_map(
        local, mesh=mesh, in_specs=placed, out_specs=(P("rows"), P("cols")), check_vma=False
    )
```

profile of v0, /device:TPU:1, one launch (start us, length us, event | category | flops | bytes accessed | tf_op | source)
XLA Modules:
  0.0 1307.4 jit_solution(6303000346675965485)
XLA Ops:
  10.1 76.1 %all-gather.2.cloned.1.call-done = bf16[4096,128]{1,0:T(8,128)(2,1)} async-done(((bf16[128,128]{1,0:T(8,128)(2,1)}), bf16[4096,128]{1,0:T(8,128)(2,1)}) %all-gather.2.cloned.1.call-update) | async-done | bytes 1048592 | tf_op jit(solution)/shard_map/all_gather | solution.py:71
  86.2 51.2 %while.69 = (s32[]{:T(128)}, f32[16,2,256]{2,1,0:T(2,128)S(1)}, f32[2048]{0:T(1024)}, f32[2048]{0:T(1024)}, bf16[16,256,128]{2,1,0:T(8,128)(2,1)}, /*index=5*/f3...) while((s32[]{:T(128)}, f32[16,2,256]{2,1,0:T(2,128)S(1)}, f32[2048]{0:T(1024)}, f32[2048]{0:T(1024)}, ...), condition=%wide.region_5.6_spmd, body=%wide.region_1.5_spmd.sunk | while | flops 139034368 | bytes 4884061 | solution.py:29
  137.4 112.5 %pmax.42 = f32[4096]{0:T(1024)S(1)} all-reduce(f32[4096]{0:T(1024)S(1)} %bitcast.143), channel_id=1, replica_groups=mesh['rows'=8,'cols'=32] {'cols'}, use_global_device_ids=true, to_apply=%region_6.7 | all-reduce | flops 4096 | bytes 32768 | tf_op jit(solution)/shard_map/pmax | solution.py:55
  249.9 110.6 %psum.42 = f32[4096]{0:T(1024)S(1)} all-reduce(f32[4096]{0:T(1024)S(1)} %exponential_multiply_fusion.2), channel_id=1, replica_groups=mesh['rows'=8,'cols'=32] {'cols'}, use_global_device_ids=true, to_apply=%region_7.8 | all-reduce | flops 4096 | bytes 32768 | tf_op jit(solution)/shard_map/psum | solution.py:56
  360.5 49.6 %while.72 = (s32[]{:T(128)}, f32[2048]{0:T(1024)S(1)}, f32[2048]{0:T(1024)S(1)}, f32[16,256]{1,0:T(8,128)S(1)}, f32[16,256]{1,0:T(8,128)S(1)}, /*index=5*/bf16[1...) while((s32[]{:T(128)}, f32[2048]{0:T(1024)S(1)}, ...), condition=%wide.region_12.13_spmd.clone, body=%wide.region_8.12_spmd.clone.sunk | while | flops 139044608 | bytes 4973176 | solution.py:50
  410.1 72.0 %pmax.43 = f32[2048]{0:T(1024)S(1)} all-reduce(f32[2048]{0:T(1024)S(1)} %get-tuple-element.243), channel_id=1, replica_groups=mesh['rows'=8,'cols'=32] {'rows'}, use_global_device_ids=true, to_apply=%region_13.14 | all-reduce | flops 2048 | bytes 16384 | tf_op jit(solution)/shard_map/pmax | solution.py:61
  482.1 12.7 psum.43
  494.8 51.9 %while.70 = (s32[]{:T(128)}, f32[16,2,256]{2,1,0:T(2,128)S(1)}, f32[2048]{0:T(1024)S(1)}, f32[2048]{0:T(1024)S(1)}, bf16[16,256,128]{2,1,0:T(8,128)(2,1)}, /*ind...) while((s32[]{:T(128)}, f32[16,2,256]{2,1,0:T(2,128)S(1)}, f32[2048]{0:T(1024)S(1)}, ...), condition=%wide.region_19.20_spmd, body=%wide.region_15.19_spmd.sunk | while | flops 139034368 | bytes 4884061 | solution.py:29
  495.8 1.8 fusion.85
  499.0 1.8 fusion.85
  502.3 1.8 fusion.85
  508.8 1.8 fusion.85
  512.0 1.8 fusion.85
  515.3 1.8 fusion.85
  518.5 1.8 fusion.85
  525.0 1.8 fusion.85
  528.3 1.8 fusion.85
  531.5 1.8 fusion.85
  534.7 1.8 fusion.85
  541.2 1.8 fusion.85
  544.5 1.8 fusion.85
  546.8 109.9 %pmax.44 = f32[4096]{0:T(1024)S(1)} all-reduce(f32[4096]{0:T(1024)S(1)} %bitcast.145), channel_id=1, replica_groups=mesh['rows'=8,'cols'=32] {'cols'}, use_global_device_ids=true, to_apply=%region_20.21 | all-reduce | flops 4096 | bytes 32768 | tf_op jit(solution)/shard_map/pmax | solution.py:55
  656.7 110.3 %psum.44 = f32[4096]{0:T(1024)S(1)} all-reduce(f32[4096]{0:T(1024)S(1)} %exponential_multiply_fusion.1), channel_id=1, replica_groups=mesh['rows'=8,'cols'=32] {'cols'}, use_global_device_ids=true, to_apply=%region_21.22 | all-reduce | flops 4096 | bytes 32768 | tf_op jit(solution)/shard_map/psum | solution.py:56
  767.0 49.6 %while.73 = (s32[]{:T(128)}, f32[2048]{0:T(1024)S(1)}, f32[2048]{0:T(1024)S(1)}, f32[16,256]{1,0:T(8,128)S(1)}, f32[16,256]{1,0:T(8,128)S(1)}, /*index=5*/bf16[1...) while((s32[]{:T(128)}, f32[2048]{0:T(1024)S(1)}, ...), condition=%wide.region_26.27_spmd.clone, body=%wide.region_22.26_spmd.clone.sunk | while | flops 139044608 | bytes 4973176 | solution.py:50
  816.6 67.8 %pmax.45 = f32[2048]{0:T(1024)S(1)} all-reduce(f32[2048]{0:T(1024)S(1)} %get-tuple-element.246), channel_id=1, replica_groups=mesh['rows'=8,'cols'=32] {'rows'}, use_global_device_ids=true, to_apply=%region_27.28 | all-reduce | flops 2048 | bytes 16384 | tf_op jit(solution)/shard_map/pmax | solution.py:61
  884.4 12.7 psum.45
  897.2 51.8 %while.71 = (s32[]{:T(128)}, f32[16,2,256]{2,1,0:T(2,128)S(1)}, f32[2048]{0:T(1024)S(1)}, f32[2048]{0:T(1024)S(1)}, bf16[16,256,128]{2,1,0:T(8,128)(2,1)}, /*ind...) while((s32[]{:T(128)}, f32[16,2,256]{2,1,0:T(2,128)S(1)}, f32[2048]{0:T(1024)S(1)}, ...), condition=%wide.region_33.34_spmd, body=%wide.region_29.33_spmd.sunk | while | flops 139034368 | bytes 4884061 | solution.py:29
  949.0 109.9 %pmax.46 = f32[4096]{0:T(1024)S(1)} all-reduce(f32[4096]{0:T(1024)S(1)} %bitcast.147), channel_id=1, replica_groups=mesh['rows'=8,'cols'=32] {'cols'}, use_global_device_ids=true, to_apply=%region_34.35 | all-reduce | flops 4096 | bytes 32768 | tf_op jit(solution)/shard_map/pmax | solution.py:55
  1059.0 110.3 %psum.46 = f32[4096]{0:T(1024)S(1)} all-reduce(f32[4096]{0:T(1024)S(1)} %exponential_multiply_fusion), channel_id=1, replica_groups=mesh['rows'=8,'cols'=32] {'cols'}, use_global_device_ids=true, to_apply=%region_35.36 | all-reduce | flops 4096 | bytes 32768 | tf_op jit(solution)/shard_map/psum | solution.py:56
  1169.9 49.6 %while.74 = (s32[]{:T(128)}, f32[2048]{0:T(1024)S(1)}, f32[2048]{0:T(1024)S(1)}, f32[16,256]{1,0:T(8,128)S(1)}, f32[16,256]{1,0:T(8,128)S(1)}, /*index=5*/bf16[1...) while((s32[]{:T(128)}, f32[2048]{0:T(1024)S(1)}, ...), condition=%wide.region_40.41_spmd.clone, body=%wide.region_36.40_spmd.clone.sunk | while | flops 139044608 | bytes 4973176 | solution.py:50
  1219.5 67.8 %pmax.47 = f32[2048]{0:T(1024)S(1)} all-reduce(f32[2048]{0:T(1024)S(1)} %get-tuple-element.249), channel_id=1, replica_groups=mesh['rows'=8,'cols'=32] {'rows'}, use_global_device_ids=true, to_apply=%region_41.42 | all-reduce | flops 2048 | bytes 16384 | tf_op jit(solution)/shard_map/pmax | solution.py:61
  1287.3 12.7 psum.47
  (550 shorter events, 280.8 us)
Async XLA Ops:
  7.2 79.0 %all-gather.2.cloned.1.call-start = ((), (), s32[]{:S(2)}) async-start(), calls=%async_computation | async-start | bytes 1081344 | tf_op jit(solution)/shard_map/all_gather | solution.py:71
  360.5 134.3 %copy-start.1 = (f32[2048]{0:T(1024)S(1)}, f32[2048]{0:T(1024)}, u32[]{:S(2)}) copy-start(f32[2048]{0:T(1024)} %get-tuple-element.941) | copy-start | bytes 24580
  1169.3 0.6 copy-start
Sparse Core Ops, SparseCore 0:
  10.6 75.5 all-gather.1
where the time goes:
time: 1310 us
  blocking collectives  909 us (69%)
  matrix products  170 us (13%)
  other arithmetic  131 us (10%)
  waiting for transfers between devices  76.8 us (6%)
  between operations  14.3 us (1%)
    pmax x3, blocking collectives, join_cols(): upper = lax.pmax(top, 'cols')  332 us
    psum x3, blocking collectives, join_cols(): whole = lax.psum(total * jnp.exp(top - upper), 'cols')  331 us
    pmax x3, blocking collectives, join_rows(): upper = lax.pmax(top, 'rows')  208 us
    dot_general x96, matrix products, inner_cost(): lax.dot_general(xb, targets, (((1,), (1,)), ((), ())), preferred_element_...  170 us
    reduce_sum x96, other arithmetic, inner_cost(): xnorm = jnp.sum(jnp.square(xb.astype(jnp.float32)), axis=1)  91.7 us
    all_gather x1, waiting for transfers between devices, local(): gathered = lax.all_gather(logged, 'cols', axis=0, tiled=True)  76.1 us
    psum x3, blocking collectives, join_rows(): whole = lax.psum(total * jnp.exp(top - upper), 'rows')  38 us
  transfers between devices with their start and end apart: 1, of which 1 were waited for; matrix products, arithmetic and copies ran while one was open for 0% of the time, Pallas kernels for 0%

commit v1 on v0

--- a/solution.py
+++ b/solution.py
@@ -68,7 +68,9 @@
     width = targets.shape[0]
     pot_g = start_g
     pot_f = jnp.zeros(log_a.shape, jnp.float32)
-    gathered = lax.all_gather(logged, "cols", axis=0, tiled=True)
+    gathered = jnp.concatenate(
+        lax.all_to_all(jnp.stack([logged] * lax.axis_size("cols")), "cols", 0, 0), axis=0
+    )
     for step in range(ITERS):
         partial_value = row_partial(gathered, targets, tnorm, log_b, pot_g)
         pot_f = join_cols(partial_value[0], partial_value[1])

time: 1310 us -> 1170 us (0.89)
  other arithmetic: 131 us -> 51.2 us
  waiting for transfers between devices: 76.8 us -> 23.2 us
  between operations: 14.3 us -> 0.98 us
    reduce_sum x96, other arithmetic: 91.7 us -> 11.4 us  [inner_cost(): xnorm = jnp.sum(jnp.square(xb.astype(jnp.float32)), axis=1)]
    all_gather x1 -> x0, waiting for transfers between devices: 76.1 us -> none  [local(): gathered = lax.all_gather(logged, 'cols', axis=0, tiled=True)]
    all_to_all x0 -> x1, waiting for transfers between devices: none -> 23.2 us  [local(): lax.all_to_all(jnp.stack([logged] * lax.axis_size('cols')), 'cols', 0, 0)]
where the time goes in v1:
time: 1170 us
  blocking collectives  909 us (78%)
  matrix products  167 us (14%)
  other arithmetic  51.2 us (4%)
  waiting for transfers between devices  23.2 us (2%)
  starting transfers between devices  11.9 us (1%)
    pmax x3, blocking collectives, join_cols(): upper = lax.pmax(top, 'cols')  335 us
    psum x3, blocking collectives, join_cols(): whole = lax.psum(total * jnp.exp(top - upper), 'cols')  331 us
    pmax x3, blocking collectives, join_rows(): upper = lax.pmax(top, 'rows')  205 us
    dot_general x96, matrix products, inner_cost(): lax.dot_general(xb, targets, (((1,), (1,)), ((), ())), preferred_element_...  167 us
    psum x3, blocking collectives, join_rows(): whole = lax.psum(total * jnp.exp(top - upper), 'rows')  37.8 us
  transfers between devices with their start and end apart: 1, of which 1 were waited for; matrix products, arithmetic and copies ran while one was open for 0% of the time, Pallas kernels for 0%

profile of v1, /device:TPU:1, one launch (start us, length us, event | category | flops | bytes accessed | tf_op | source)
XLA Modules:
  0.0 1169.8 jit_solution(619571775580261562)
XLA Ops:
  0.7 2.0 stack.20
  2.7 11.9 %all-to-all-start = ((bf16[32,128,128]{2,1,0:T(8,128)(2,1)}), bf16[32,128,128]{2,1,0:T(8,128)(2,1)S(1)}, u32[]{:S(2)}, u32[]{:S(2)}) async-start(bf16[32,128,128]{2,1,0:T(8,128)(2,1)} %stack.20), calls=%async_computation | async-start | bytes 2097152 | tf_op jit(solution)/shard_map/all_to_all | solution.py:72
  16.0 23.2 %all-to-all-done = bf16[32,128,128]{2,1,0:T(8,128)(2,1)S(1)} async-done(((bf16[32,128,128]{2,1,0:T(8,128)(2,1)}), bf16[32,128,128]{2,1,0:T(8,128)(2,1)S(1)}, u32[]{:S(2)}, u32[]{:S(2)}) %all-to-all-start) | async-done | bytes 1048608 | tf_op jit(solution)/shard_map/all_to_all | solution.py:72
  39.2 37.9 %while.69 = (s32[]{:T(128)}, f32[16,2,256]{2,1,0:T(2,128)S(1)}, f32[2048]{0:T(1024)S(1)}, f32[2048]{0:T(1024)S(1)}, bf16[16,256,128]{2,1,0:T(8,128)(2,1)S(1)}, /...) while((s32[]{:T(128)}, f32[16,2,256]{2,1,0:T(2,128)S(1)}, f32[2048]{0:T(1024)S(1)}, ...), condition=%wide.region_5.6_spmd, body=%wide.region_1.5_spmd.sunk | while | flops 139034368 | bytes 4883553 | solution.py:29
  77.1 114.7 %pmax.42 = f32[4096]{0:T(1024)S(1)} all-reduce(f32[4096]{0:T(1024)S(1)} %bitcast.143), channel_id=1, replica_groups=mesh['rows'=8,'cols'=32] {'cols'}, use_global_device_ids=true, to_apply=%region_6.7 | all-reduce | flops 4096 | bytes 32768 | tf_op jit(solution)/shard_map/pmax | solution.py:55
  191.8 110.6 %psum.42 = f32[4096]{0:T(1024)S(1)} all-reduce(f32[4096]{0:T(1024)S(1)} %exponential_multiply_fusion.2), channel_id=1, replica_groups=mesh['rows'=8,'cols'=32] {'cols'}, use_global_device_ids=true, to_apply=%region_7.8 | all-reduce | flops 4096 | bytes 32768 | tf_op jit(solution)/shard_map/psum | solution.py:56
  302.4 35.6 %while.72 = (s32[]{:T(128)}, f32[2048]{0:T(1024)S(1)}, f32[2048]{0:T(1024)S(1)}, f32[16,256]{1,0:T(8,128)S(1)}, f32[16,256]{1,0:T(8,128)S(1)}, /*index=5*/bf16[1...) while((s32[]{:T(128)}, f32[2048]{0:T(1024)S(1)}, ...), condition=%wide.region_12.13_spmd.clone, body=%wide.region_8.12_spmd.clone.sunk | while | flops 139044608 | bytes 4972668 | solution.py:50
  338.0 69.4 %pmax.43 = f32[2048]{0:T(1024)S(1)} all-reduce(f32[2048]{0:T(1024)S(1)} %get-tuple-element.243), channel_id=1, replica_groups=mesh['rows'=8,'cols'=32] {'rows'}, use_global_device_ids=true, to_apply=%region_13.14 | all-reduce | flops 2048 | bytes 16384 | tf_op jit(solution)/shard_map/pmax | solution.py:61
  407.5 12.5 %psum.43 = f32[2048]{0:T(1024)S(1)} all-reduce(f32[2048]{0:T(1024)S(1)} %exponential_multiply_fusion.5), channel_id=1, replica_groups=mesh['rows'=8,'cols'=32] {'rows'}, use_global_device_ids=true, to_apply=%region_14.15 | all-reduce | flops 2048 | bytes 16384 | tf_op jit(solution)/shard_map/psum | solution.py:62
  420.0 37.9 %while.70 = (s32[]{:T(128)}, f32[16,2,256]{2,1,0:T(2,128)S(1)}, f32[2048]{0:T(1024)S(1)}, f32[2048]{0:T(1024)S(1)}, bf16[16,256,128]{2,1,0:T(8,128)(2,1)S(1)}, /...) while((s32[]{:T(128)}, f32[16,2,256]{2,1,0:T(2,128)S(1)}, f32[2048]{0:T(1024)S(1)}, ...), condition=%wide.region_19.20_spmd, body=%wide.region_15.19_spmd.sunk | while | flops 139034368 | bytes 4883553 | solution.py:29
  422.5 1.8 fusion.85
  457.9 110.0 %pmax.44 = f32[4096]{0:T(1024)S(1)} all-reduce(f32[4096]{0:T(1024)S(1)} %bitcast.145), channel_id=1, replica_groups=mesh['rows'=8,'cols'=32] {'cols'}, use_global_device_ids=true, to_apply=%region_20.21 | all-reduce | flops 4096 | bytes 32768 | tf_op jit(solution)/shard_map/pmax | solution.py:55
  567.9 110.3 %psum.44 = f32[4096]{0:T(1024)S(1)} all-reduce(f32[4096]{0:T(1024)S(1)} %exponential_multiply_fusion.1), channel_id=1, replica_groups=mesh['rows'=8,'cols'=32] {'cols'}, use_global_device_ids=true, to_apply=%region_21.22 | all-reduce | flops 4096 | bytes 32768 | tf_op jit(solution)/shard_map/psum | solution.py:56
  678.2 35.6 %while.73 = (s32[]{:T(128)}, f32[2048]{0:T(1024)S(1)}, f32[2048]{0:T(1024)S(1)}, f32[16,256]{1,0:T(8,128)S(1)}, f32[16,256]{1,0:T(8,128)S(1)}, /*index=5*/bf16[1...) while((s32[]{:T(128)}, f32[2048]{0:T(1024)S(1)}, ...), condition=%wide.region_26.27_spmd.clone, body=%wide.region_22.26_spmd.clone.sunk | while | flops 139044608 | bytes 4972668 | solution.py:50
  713.8 67.8 %pmax.45 = f32[2048]{0:T(1024)S(1)} all-reduce(f32[2048]{0:T(1024)S(1)} %get-tuple-element.246), channel_id=1, replica_groups=mesh['rows'=8,'cols'=32] {'rows'}, use_global_device_ids=true, to_apply=%region_27.28 | all-reduce | flops 2048 | bytes 16384 | tf_op jit(solution)/shard_map/pmax | solution.py:61
  781.7 12.7 %psum.45 = f32[2048]{0:T(1024)S(1)} all-reduce(f32[2048]{0:T(1024)S(1)} %exponential_multiply_fusion.4), channel_id=1, replica_groups=mesh['rows'=8,'cols'=32] {'rows'}, use_global_device_ids=true, to_apply=%region_28.29 | all-reduce | flops 2048 | bytes 16384 | tf_op jit(solution)/shard_map/psum | solution.py:62
  794.4 37.9 %while.71 = (s32[]{:T(128)}, f32[16,2,256]{2,1,0:T(2,128)S(1)}, f32[2048]{0:T(1024)S(1)}, f32[2048]{0:T(1024)S(1)}, bf16[16,256,128]{2,1,0:T(8,128)(2,1)S(1)}, /...) while((s32[]{:T(128)}, f32[16,2,256]{2,1,0:T(2,128)S(1)}, f32[2048]{0:T(1024)S(1)}, ...), condition=%wide.region_33.34_spmd, body=%wide.region_29.33_spmd.sunk | while | flops 139034368 | bytes 4883553 | solution.py:29
  794.5 1.8 fusion.88
  796.9 1.8 fusion.88
  801.6 1.8 fusion.88
  804.0 1.8 fusion.88
  808.7 1.8 fusion.88
  811.1 1.8 fusion.88
  815.8 1.8 fusion.88
  818.2 1.8 fusion.88
  822.9 1.8 fusion.88
  825.3 1.8 fusion.88
  832.3 109.9 %pmax.46 = f32[4096]{0:T(1024)S(1)} all-reduce(f32[4096]{0:T(1024)S(1)} %bitcast.147), channel_id=1, replica_groups=mesh['rows'=8,'cols'=32] {'cols'}, use_global_device_ids=true, to_apply=%region_34.35 | all-reduce | flops 4096 | bytes 32768 | tf_op jit(solution)/shard_map/pmax | solution.py:55
  942.2 110.3 %psum.46 = f32[4096]{0:T(1024)S(1)} all-reduce(f32[4096]{0:T(1024)S(1)} %exponential_multiply_fusion), channel_id=1, replica_groups=mesh['rows'=8,'cols'=32] {'cols'}, use_global_device_ids=true, to_apply=%region_35.36 | all-reduce | flops 4096 | bytes 32768 | tf_op jit(solution)/shard_map/psum | solution.py:56
  1053.1 35.6 %while.74 = (s32[]{:T(128)}, f32[2048]{0:T(1024)S(1)}, f32[2048]{0:T(1024)S(1)}, f32[16,256]{1,0:T(8,128)S(1)}, f32[16,256]{1,0:T(8,128)S(1)}, /*index=5*/bf16[1...) while((s32[]{:T(128)}, f32[2048]{0:T(1024)S(1)}, ...), condition=%wide.region_40.41_spmd.clone, body=%wide.region_36.40_spmd.clone.sunk | while | flops 139044608 | bytes 4972668 | solution.py:50
  1088.7 67.8 %pmax.47 = f32[2048]{0:T(1024)S(1)} all-reduce(f32[2048]{0:T(1024)S(1)} %get-tuple-element.249), channel_id=1, replica_groups=mesh['rows'=8,'cols'=32] {'rows'}, use_global_device_ids=true, to_apply=%region_41.42 | all-reduce | flops 2048 | bytes 16384 | tf_op jit(solution)/shard_map/pmax | solution.py:61
  1156.5 12.7 %psum.47 = f32[2048]{0:T(1024)S(1)} all-reduce(f32[2048]{0:T(1024)S(1)} %exponential_multiply_fusion.3), channel_id=1, replica_groups=mesh['rows'=8,'cols'=32] {'rows'}, use_global_device_ids=true, to_apply=%region_42.43 | all-reduce | flops 2048 | bytes 16384 | tf_op jit(solution)/shard_map/psum | solution.py:62
  (554 shorter events, 200.1 us)
Async XLA Ops:
  0.6 14.0 %copy-start.1 = (f32[4096]{0:T(1024)S(1)}, f32[4096]{0:T(1024)}, u32[]{:S(2)}) copy-start(f32[4096]{0:T(1024)} %param.19) | copy-start | bytes 49156
  0.6 38.5 %copy-start.3 = (f32[2048]{0:T(1024)S(1)}, f32[2048]{0:T(1024)}, u32[]{:S(2)}) copy-start(f32[2048]{0:T(1024)} %param.20) | copy-start | bytes 24580
  0.7 38.5 %copy-start.2 = (f32[2048]{0:T(1024)S(1)}, f32[2048]{0:T(1024)}, u32[]{:S(2)}) copy-start(f32[2048]{0:T(1024)} %param.21) | copy-start | bytes 24580
  2.7 36.5 %all-to-all-start = ((bf16[32,128,128]{2,1,0:T(8,128)(2,1)}), bf16[32,128,128]{2,1,0:T(8,128)(2,1)S(1)}, u32[]{:S(2)}, u32[]{:S(2)}) async-start(bf16[32,128,128]{2,1,0:T(8,128)(2,1)} %stack.20), calls=%async_computation | async-start | bytes 2097152 | tf_op jit(solution)/shard_map/all_to_all | solution.py:72
  1052.5 0.6 copy-start
